TPU v7x, 256 devices: a whole 4x4x8 slice. The times are simulated.
256 devices in a mesh: seq: 128 (over z, x_lo, y, core), dp: 2 (over x_hi).
Axes of the slice: x: 4 (x_hi: 2, x_lo: 2; x = x_hi * 2 + x_lo), y: 4, z: 8, core: 2. Of those that a mesh axis runs over, the one named last changes fastest.
Arguments:
- genome: bfloat16 [2, 262144, 512], P('dp', 'seq'), may hold values from -6 to 6
- conv_weight: bfloat16 [3, 512, 512], replicated, may hold values from -0.15625 to 0.15625
- upstream: bfloat16 [2, 262144, 512], P('dp', 'seq'), may hold values from -6 to 6
Outputs:
- output: bfloat16 [2, 262144, 512], P('dp', 'seq')
- grad_genome: bfloat16 [2, 262144, 512], P('dp', 'seq')
- grad_weight: float32 [3, 512, 512], replicated
All inputs are finite; a program needn't handle non-finite values.
Results may differ from a plain program's by a relative error of at most 0.0035.
Values may be sent and summed in bfloat16 or wider, within the bound.
A program may use at most 128 MiB of HBM per device.

v0:
```python
import jax
import jax.numpy as jnp
from jax import lax
from jax.sharding import PartitionSpec as P

DILATION_BINS = 4096


def passed_along(value, axis, steps):
    count = lax.axis_size(axis)
    leading, last = (max(0, -steps), min(count, count - steps))
    return lax.ppermute(value, axis, [(source, source + steps) for source in range(leading, last)])


def mixing(left, right):
    return jnp.einsum("gbc,cd->gbd", left, right, preferred_element_type=jnp.float32)


def mixing_back(left, right):
    return jnp.einsum("gbd,cd->gbc", left, right, preferred_element_type=jnp.float32)


def outer_sum(left, right):
    return jnp.einsum("gbc,gbd->cd", left, right, preferred_element_type=jnp.float32)


def layer_arithmetic(
    genome, upstream, act, act_prev, act_next, up_prev, up_next, slope_fn, conv_weight
):
    conv = (
        mixing(act_prev, conv_weight[0])
        + mixing(act, conv_weight[1])
        + mixing(act_next, conv_weight[2])
    )
    output = (genome.astype(jnp.float32) + conv).astype(jnp.bfloat16)
    grad_act = (
        mixing_back(up_next, conv_weight[0])
        + mixing_back(upstream, conv_weight[1])
        + mixing_back(up_prev, conv_weight[2])
    )
    grad_genome = (upstream.astype(jnp.float32) + slope_fn(grad_act)[0]).astype(jnp.bfloat16)
    partial_gradient = jnp.stack(
        [outer_sum(act_prev, upstream), outer_sum(act, upstream), outer_sum(act_next, upstream)]
    )
    return (output, grad_genome, partial_gradient)


def per_device(genome, conv_weight, upstream):
    channel_groups, bin_positions, chans = genome.shape
    act_full, slope_fn = jax.vjp(jax.nn.gelu, genome.astype(jnp.float32))
    act = act_full.astype(jnp.bfloat16)
    tap_offset = DILATION_BINS // bin_positions
    act_prev, up_prev = passed_along((act, upstream), "seq", tap_offset)
    act_next, up_next = passed_along((act, upstream), "seq", -tap_offset)
    output, grad_genome, partial_gradient = layer_arithmetic(
        genome, upstream, act, act_prev, act_next, up_prev, up_next, slope_fn, conv_weight
    )
    grad_weight = lax.psum(partial_gradient, ("seq", "dp"))
    return (output, grad_genome, grad_weight)


def solution(mesh):
    return jax.shard_map(
        per_device,
        mesh=mesh,
        in_specs=(P("dp", "seq", None), P(), P("dp", "seq", None)),
        out_specs=(P("dp", "seq", None), P("dp", "seq", None), P()),
        check_vma=False,
    )
```

profile of v0, /device:TPU:1, one launch (start us, length us, event | category | flops | bytes accessed | tf_op | source)
XLA Modules:
  0.0 357.1 jit_solution(11124248696219987834)
XLA Ops:
  7.2 0.0 all-reduce.2.cloned.1.call-start
  7.2 3.1 fusion.8
  10.4 4.3 %collective-permute-start = (bf16[1,2048,512]{2,1,0:T(8,128)(2,1)S(1)}, bf16[1,2048,512]{2,1,0:T(8,128)(2,1)S(1)}, u32[]{:S(2)}, u32[]{:S(2)}) collective-permute-start(bf16[1,2048,512]{2,1,0:T(8,128)(2,1)S(1)} %fusion.8), channel_id=1, source_target_pairs={{0,4},{2,6},{4,8},{6,10},{8,12},{10,14},{12,16},{14,18},{16,20},{1... | collective-permute-start | bytes 6291464 | tf_op jit(solution)/shard_map/ppermute | solution.py:12
  14.7 1.3 collective-permute-start.1
  16.0 1.3 collective-permute-start.2
  17.3 6.1 %collective-permute-start.3 = (bf16[1,2048,512]{2,1,0:T(8,128)(2,1)}, bf16[1,2048,512]{2,1,0:T(8,128)(2,1)}, u32[]{:S(2)}, u32[]{:S(2)}) collective-permute-start(bf16[1,2048,512]{2,1,0:T(8,128)(2,1)} %param.5), channel_id=1, source_target_pairs={{0,4},{2,6},{4,8},{6,10},{8,12},{10,14},{12,16},{14,18},{16,20},{1... | collective-permute-start | bytes 6291464 | tf_op jit(solution)/shard_map/ppermute | solution.py:12
  23.3 4.8 %fusion.21 = f32[2048,512]{1,0:T(8,128)} fusion(bf16[1,2048,512]{2,1,0:T(8,128)(2,1)} %param.5, bf16[3,512,512]{2,1,0:T(8,128)(2,1)S(1)} %copy-done.4), kind=kOutput, calls=%fused_computation.29 | convolution fusion | flops 1073741824 | bytes 6815744 | tf_op jit(solution)/shard_map/gbd,cd->gbc/dot_general | solution.py:20
  28.2 3.6 %fusion.31 = f32[2048,512]{1,0:T(8,128)} fusion(bf16[3,512,512]{2,1,0:T(8,128)(2,1)S(1)} %copy-done.4, bf16[1,2048,512]{2,1,0:T(8,128)(2,1)S(1)} %copy-done.1), kind=kOutput, calls=%fused_computation.37 | convolution fusion | flops 1084227584 | bytes 6815744 | tf_op jit(solution)/shard_map/gbc,cd->gbd/dot_general | solution.py:16
  31.8 3.5 fusion.43
  35.3 23.5 %collective-permute-done = bf16[1,2048,512]{2,1,0:T(8,128)(2,1)S(1)} collective-permute-done((bf16[1,2048,512]{2,1,0:T(8,128)(2,1)S(1)}, bf16[1,2048,512]{2,1,0:T(8,128)(2,1)S(1)}, u32[]{:S(2)}, u32[]{:S(2)}) %collective-permute-start) | collective-permute-done | bytes 2097184 | tf_op jit(solution)/shard_map/ppermute | solution.py:12
  58.8 1.3 copy-done.3
  60.1 2.9 fusion.38
  63.0 1.3 copy-done.6
  64.3 2.9 fusion.48
  67.2 2.0 pad_maximum_fusion
  69.2 3.1 fusion.34
  72.4 0.3 copy-done.5
  72.7 0.7 copy-done.7
  73.3 3.2 fusion.9
  76.5 33.3 %collective-permute-done.2 = bf16[1,2048,512]{2,1,0:T(8,128)(2,1)} collective-permute-done((bf16[1,2048,512]{2,1,0:T(8,128)(2,1)}, bf16[1,2048,512]{2,1,0:T(8,128)(2,1)}, u32[]{:S(2)}, u32[]{:S(2)}) %collective-permute-start.2) | collective-permute-done | bytes 2097184 | tf_op jit(solution)/shard_map/ppermute | solution.py:12
  109.8 2.9 fusion.23
  112.7 6.9 %fusion.4 = bf16[1,2048,512]{2,1,0:T(8,128)(2,1)} fusion(bf16[1,2048,512]{2,1,0:T(8,128)(2,1)S(1)} %copy-done.1, f32[2048,512]{1,0:T(8,128)S(1)} %fusion.23, f32[2048,512]{1,0:T(8,128)S(1)} %copy-done, bf16[1,2048,512]{2,1,0:T(8,128)(2,1)} %param.5, bf16[1,2048,512]{2,1,0:T(8,128)(2,1)} %collective-permute-done.3, bf16[3,512,512]{2,1,0:T(8,128)(2,1)S(1)} %copy-done.5), kind=kOutput, calls=%fused_computation.10 | convolution fusion | flops 1099956224 | bytes 17301504 | tf_op jit(solution)/shard_map/gbd,cd->gbc/dot_general | solution.py:20
  119.6 226.8 %all-reduce.2.cloned.1.call-done = f32[3,512,512]{2,1,0:T(8,128)} async-done(((f32[3,512,512]{2,1,0:T(8,128)}), f32[3,512,512]{2,1,0:T(8,128)}) %all-reduce.2.cloned.1.call-update) | async-done | bytes 3145744 | tf_op jit(solution)/shard_map/psum | solution.py:58
  346.4 3.9 %copy.7 = f32[3,512,512]{2,1,0:T(8,128)} copy(f32[3,512,512]{2,1,0:T(8,128)} %all-reduce.2.cloned.1.call-done) | data formatting | bytes 6291456
  (15 shorter events, 0.1 us)
Async XLA Ops:
  7.2 339.3 %all-reduce.2.cloned.1.call-start = ((), (), s32[]{:S(2)}) async-start(), calls=%async_computation | async-start | bytes 6291456 | tf_op jit(solution)/shard_map/psum | solution.py:58
  7.2 16.1 %copy-start.4 = (bf16[3,512,512]{2,1,0:T(8,128)(2,1)S(1)}, bf16[3,512,512]{2,1,0:T(8,128)(2,1)}, u32[]{:S(2)}) copy-start(bf16[3,512,512]{2,1,0:T(8,128)(2,1)} %param.4) | copy-start | bytes 4718596
  10.4 17.8 %copy-start.1 = (bf16[1,2048,512]{2,1,0:T(8,128)(2,1)S(1)}, bf16[1,2048,512]{2,1,0:T(8,128)(2,1)}, u32[]{:S(2)}) copy-start(bf16[1,2048,512]{2,1,0:T(8,128)(2,1)} %param.3) | copy-start | bytes 6291460
  10.4 48.5 %collective-permute-start = (bf16[1,2048,512]{2,1,0:T(8,128)(2,1)S(1)}, bf16[1,2048,512]{2,1,0:T(8,128)(2,1)S(1)}, u32[]{:S(2)}, u32[]{:S(2)}) collective-permute-start(bf16[1,2048,512]{2,1,0:T(8,128)(2,1)S(1)} %fusion.8), channel_id=1, source_target_pairs={{0,4},{2,6},{4,8},{6,10},{8,12},{10,14},{12,16},{14,18},{16,20},{1... | collective-permute-start | bytes 6291464 | tf_op jit(solution)/shard_map/ppermute | solution.py:12
  14.7 48.4 %collective-permute-start.1 = (bf16[1,2048,512]{2,1,0:T(8,128)(2,1)S(1)}, bf16[1,2048,512]{2,1,0:T(8,128)(2,1)S(1)}, u32[]{:S(2)}, u32[]{:S(2)}) collective-permute-start(bf16[1,2048,512]{2,1,0:T(8,128)(2,1)S(1)} %fusion.8), channel_id=1, source_target_pairs={{4,0},{6,2},{8,4},{10,6},{12,8},{14,10},{16,12},{18,14},{20,16},{2... | collective-permute-start | bytes 6291464 | tf_op jit(solution)/shard_map/ppermute | solution.py:12
  16.0 93.8 %collective-permute-start.2 = (bf16[1,2048,512]{2,1,0:T(8,128)(2,1)}, bf16[1,2048,512]{2,1,0:T(8,128)(2,1)}, u32[]{:S(2)}, u32[]{:S(2)}) collective-permute-start(bf16[1,2048,512]{2,1,0:T(8,128)(2,1)} %param.5), channel_id=1, source_target_pairs={{4,0},{6,2},{8,4},{10,6},{12,8},{14,10},{16,12},{18,14},{20,16},{2... | collective-permute-start | bytes 6291464 | tf_op jit(solution)/shard_map/ppermute | solution.py:12
  17.3 95.4 %collective-permute-start.3 = (bf16[1,2048,512]{2,1,0:T(8,128)(2,1)}, bf16[1,2048,512]{2,1,0:T(8,128)(2,1)}, u32[]{:S(2)}, u32[]{:S(2)}) collective-permute-start(bf16[1,2048,512]{2,1,0:T(8,128)(2,1)} %param.5), channel_id=1, source_target_pairs={{0,4},{2,6},{4,8},{6,10},{8,12},{10,14},{12,16},{14,18},{16,20},{1... | collective-permute-start | bytes 6291464 | tf_op jit(solution)/shard_map/ppermute | solution.py:12
  58.8 1.3 copy-start.3
  63.0 1.3 copy-start.6
  69.2 3.1 copy-start.2
  69.2 3.5 copy-start.5
  69.2 4.1 %copy-start.7 = (bf16[1,2048,512]{2,1,0:T(8,128)(2,1)S(1)}, bf16[1,2048,512]{2,1,0:T(8,128)(2,1)}, u32[]{:S(2)}) copy-start(bf16[1,2048,512]{2,1,0:T(8,128)(2,1)} %copy-done.6) | copy-start | bytes 6291460
  76.5 36.2 %copy-start = (f32[2048,512]{1,0:T(8,128)S(1)}, f32[2048,512]{1,0:T(8,128)}, u32[]{:S(2)}) copy-start(f32[2048,512]{1,0:T(8,128)} %fusion.21) | copy-start | bytes 12582916
Sparse Core Ops, SparseCore 0:
  69.3 277.0 all-reduce.1
where the time goes:
time: 358 us; the launch traced here: 357 us
  waiting for transfers between devices  284 us (79%)
  matrix products  33.7 us (9%)
  between operations  14.2 us (4%)
  starting transfers between devices  13 us (4%)
  local copies, waits for them, and re-layouts  7.49 us (2%)
  other arithmetic  5.11 us (1%)
    psum x1, waiting for transfers between devices, per_device(): grad_weight = lax.psum(partial_gradient, ('seq', 'dp'))  227 us
    ppermute x4, waiting for transfers between devices, passed_along(): lax.ppermute(value, axis, [(source, source + steps) for source in range(l...  56.8 us
    dot_general x3, matrix products, mixing_back(): jnp.einsum('gbd,cd->gbc', left, right, preferred_element_type=jnp.float32)  14.6 us
    ppermute x4, starting transfers between devices, passed_along(): lax.ppermute(value, axis, [(source, source + steps) for source in range(l...  12.9 us
    dot_general x3, matrix products, mixing(): jnp.einsum('gbc,cd->gbd', left, right, preferred_element_type=jnp.float32)  9.9 us
    dot_general x3, matrix products, outer_sum(): jnp.einsum('gbc,gbd->cd', left, right, preferred_element_type=jnp.float32)  9.2 us
    unnamed x17, local copies, waits for them, and re-layouts  7.49 us
  transfers between devices with their start and end apart: 5, of which 3 were waited for; matrix products, arithmetic and copies ran while one was open for 10% of the time, Pallas kernels for 0%

commit v1 on v0

v1 whole, which is shorter than its diff:
```python
import functools

import jax
import jax.numpy as jnp
from jax import lax
from jax.experimental import pallas as pl
from jax.experimental.pallas import tpu as pltpu
from jax.sharding import PartitionSpec as P

MESH = pl.DeviceIdType.MESH
F32 = jnp.float32
BF16 = jnp.bfloat16
DILATION_BINS = 4096
NCH = 8
NGC = 16
AHEAD = 2
CUBIC = 0.044715
SLOPE = 0.7978845608028654


def gelu(x):
    return x * (0.5 * (1.0 + jnp.tanh(SLOPE * (x + CUBIC * (x * x * x)))))


def gelu_slope(x):
    square = x * x
    t = jnp.tanh(SLOPE * (x + CUBIC * (x * square)))
    return 0.5 * (1.0 + t) + (0.5 * SLOPE) * x * (1.0 - t * t) * (1.0 + (3.0 * CUBIC) * square)


def dot(a, b):
    return jnp.dot(a, b, preferred_element_type=F32)


def dot_nt(a, b):
    return lax.dot_general(a, b, (((1,), (1,)), ((), ())), preferred_element_type=F32)


def kernel(
    dims, hop,
    g_hbm, w_hbm, u_hbm, out_hbm, gg_hbm, gw_hbm,
    g, u, w, u_prev, u_next, g_prev, g_next, act, act_t, ob, gb,
    acc, rc, xs, rx, zs, rz, ry, ag, gwf,
    lsem, us, ur, gs, gr, osem, gsem, wsem,
    cs, cr, xss, xr, zss, zr, yss, yr, azs, azr, axs, axr, acs, acr,
):
    nz, nxl, ny, nd = dims
    nx = nxl * nd
    ns = nz * nxl * ny * 2
    bins, chans = g.shape
    rows = 3 * chans
    rx_rows = rows // nx
    rz_rows = rx_rows // nz
    ch, gch = bins // NCH, bins // NGC
    wide = chans // 2
    half = wide // 2

    s = lax.axis_index("seq")
    d = lax.axis_index("dp")
    core = lax.rem(s, 2)
    y = lax.rem(lax.div(s, 2), ny)
    xl = lax.rem(lax.div(s, 2 * ny), nxl)
    z = lax.div(s, 2 * ny * nxl)
    x = d * nxl + xl

    def at(z_, x_, y_, c_):
        return {
            "dp": lax.div(x_, nxl),
            "seq": ((z_ * nxl + lax.rem(x_, nxl)) * ny + y_) * 2 + c_,
        }

    after = {"dp": d, "seq": lax.rem(s + hop, ns)}
    before = {"dp": d, "seq": lax.rem(s + ns - hop, ns)}
    partner = at(z, x, y, 1 - core)

    def x_at(k):
        return lax.rem(x + 1 + k, nx)

    def x_from(k):
        return lax.rem(x + 2 * nx - 1 - k, nx)

    def z_at(k):
        return lax.rem(z + 1 + k, nz)

    def z_from(k):
        return lax.rem(z + 2 * nz - 1 - k, nz)

    def y_at(k):
        return lax.rem(y + 1 + k, ny)

    def y_from(k):
        return lax.rem(y + 2 * ny - 1 - k, ny)

    x_peers = [at(z, x_at(k), y, core) for k in range(nx - 1)]
    z_peers = [at(z_at(k), x, y, core) for k in range(nz - 1)]
    y_peers = [at(z, x, y_at(k), core) for k in range(ny - 1)]

    def ds(start, size, step):
        return pl.ds(pl.multiple_of(start, step), size)

    def remote(src, dst, send, recv, device):
        return pltpu.make_async_remote_copy(
            src_ref=src, dst_ref=dst, send_sem=send, recv_sem=recv, device_id=device, device_id_type=MESH
        )

    loads = [
        pltpu.make_async_copy(g_hbm, g, lsem.at[0]),
        pltpu.make_async_copy(u_hbm, u, lsem.at[1]),
        pltpu.make_async_copy(w_hbm, w, lsem.at[2]),
    ]
    for load in loads:
        load.start()

    barrier = pltpu.get_barrier_semaphore()
    greeted = [after, before, partner] + x_peers + z_peers + y_peers
    for device in greeted:
        pl.semaphore_signal(barrier, inc=1, device_id=device, device_id_type=MESH)
    pl.semaphore_wait(barrier, len(greeted))

    def up_copy(j, i, way):
        block = (ds(i * ch, ch, ch), pl.ds(j * wide, wide))
        dst = (u_prev, u_next)[way]
        return remote(
            u_hbm.at[block], dst.at[block], us.at[way, j, i], ur.at[way, j, i], (after, before)[way]
        )

    def genome_copy(i, way):
        block = ds(i * gch, gch, gch)
        dst = (g_prev, g_next)[way]
        return remote(g_hbm.at[block], dst.at[block], gs.at[way, i], gr.at[way, i], (after, before)[way])

    def send_genome(i):
        for way in range(2):
            genome_copy(i, way).start()

    for j in range(2):

        def send_up(i, _, j=j):
            for way in range(2):
                up_copy(j, i, way).start()
            return 0

        lax.fori_loop(0, NCH, send_up, 0)

    def c_copy(j, k):
        block = ds(x_at(k) * rx_rows, rx_rows, rx_rows)
        return remote(
            acc.at[j, 1 - core, block], rc.at[j, block], cs.at[j, k], cr.at[j, k], partner
        )

    def x_copy(j, k):
        block = ds(x_at(k) * rx_rows, rx_rows, rx_rows)
        return remote(xs.at[j, block], rx.at[j, k], xss.at[j, k], xr.at[j, k], x_peers[k])

    def z_copy(j, k):
        block = ds(z_at(k) * rz_rows, rz_rows, rz_rows)
        return remote(zs.at[j, block], rz.at[j, k], zss.at[j, k], zr.at[j, k], z_peers[k])

    def y_copy(j, k, slot):
        return remote(ry.at[j, slot], ry.at[j, slot], yss.at[j, k], yr.at[j, k], y_peers[k])

    def az_copy(j, k, z_):
        block = ag.at[j, core, ds(x * rx_rows + z_ * rz_rows, rz_rows, rz_rows)]
        return remote(block, block, azs.at[j, k], azr.at[j, k], z_peers[k])

    def ax_copy(j, k, x_):
        block = ag.at[j, core, ds(x_ * rx_rows, rx_rows, rx_rows)]
        return remote(block, block, axs.at[j, k], axr.at[j, k], x_peers[k])

    def ac_copy(j, c_):
        return remote(ag.at[j, c_], ag.at[j, c_], acs.at[j], acr.at[j], partner)

    def send_c(j):
        for k in range(nx):
            c_copy(j, k).start()

    def send_x(j):
        for k in range(nx - 1):
            c_copy(j, k).wait_recv()
            block = ds(x_at(k) * rx_rows, rx_rows, rx_rows)
            xs[j, block] = (acc[j, core, block] + rc[j, block]).astype(BF16)
            x_copy(j, k).start()

    def send_z(j):
        c_copy(j, nx - 1).wait_recv()
        block = ds(x * rx_rows, rx_rows, rx_rows)
        for k in range(nx - 1):
            x_copy(j, k).wait_recv()
        total = acc[j, core, block] + rc[j, block]
        for k in range(nx - 1):
            total += rx[j, k].astype(F32)
        zs[j] = total
        for k in range(nz - 1):
            z_copy(j, k).start()

    def send_y(j):
        for k in range(nz - 1):
            z_copy(j, k).wait_recv()
        total = zs[j, ds(z * rz_rows, rz_rows, rz_rows)]
        for k in range(nz - 1):
            total += rz[j, k]
        ry[j, y] = total
        for k in range(ny - 1):
            y_copy(j, k, y).start()

    def send_az(j):
        for k in range(ny - 1):
            y_copy(j, k, y_from(k)).wait_recv()
        total = ry[j, 0]
        for k in range(1, ny):
            total += ry[j, k]
        ag[j, core, ds(x * rx_rows + z * rz_rows, rz_rows, rz_rows)] = total.astype(BF16)
        for k in range(nz - 1):
            az_copy(j, k, z).start()

    def send_ax(j):
        for k in range(nz - 1):
            az_copy(j, k, z_from(k)).wait_recv()
        for k in range(nx - 1):
            ax_copy(j, k, x).start()

    def send_ac(j):
        for k in range(nx - 1):
            ax_copy(j, k, x_from(k)).wait_recv()
        ac_copy(j, core).start()

    def gw_copy(j):
        columns = pl.ds(j * wide, wide)
        return pltpu.make_async_copy(gwf.at[:, :, columns], gw_hbm.at[:, :, columns], wsem.at[j])

    def finish(j):
        ac_copy(j, 1 - core).wait_recv()
        for h in range(2):
            for k in range(3):
                gwf[k, :, pl.ds(j * wide + h * half, half)] = ag[j, h, pl.ds(k * chans, chans)].astype(F32)
        gw_copy(j).start()

    has_prev = jnp.where(s >= hop, 1.0, 0.0).astype(F32)
    has_next = jnp.where(s < ns - hop, 1.0, 0.0).astype(F32)

    for load in loads:
        load.wait()
    acc[...] = jnp.zeros_like(acc)

    def own(i, _):
        block = ds(i * gch, gch, gch)
        a = gelu(g[block].astype(F32))
        act[block] = a.astype(BF16)
        act_t[:, block] = a.T.astype(BF16)
        return 0

    lax.fori_loop(0, NGC, own, 0)

    def masked(ref, index, there):
        value = ref[index]
        return value * jnp.full(value.shape, there, F32).astype(BF16)

    def gg_copy(i):
        block = ds(i * ch, ch, ch)
        return pltpu.make_async_copy(gb.at[block], gg_hbm.at[block], gsem.at[i])

    def out_copy(i):
        block = ds(i * gch, gch, gch)
        return pltpu.make_async_copy(ob.at[block], out_hbm.at[block], osem.at[i])

    def staged(i, stages):
        for tick, stage, j in stages:
            pl.when(i == tick)(functools.partial(stage, j))

    def up_step(j, stages):
        def body(i, _):
            for way in range(2):
                up_copy(j, i, way).wait_recv()
            block = ds(i * ch, ch, ch)
            columns = pl.ds(j * wide, wide)
            left = act_t[:, block]
            for tap, right in (
                (0, masked(u_next, (block, columns), has_next)),
                (1, u[block, columns]),
                (2, masked(u_prev, (block, columns), has_prev)),
            ):
                term = dot(left, right)
                span = pl.ds(tap * chans, chans)
                acc[j, 0, span] += term[:, :half]
                acc[j, 1, span] += term[:, half:]
            if j == 1:
                own_up = u[block]
                grad_act = (
                    dot_nt(masked(u_next, block, has_next), w[0])
                    + dot_nt(own_up, w[1])
                    + dot_nt(masked(u_prev, block, has_prev), w[2])
                )
                slope = gelu_slope(g[block].astype(F32))
                gb[block] = (own_up.astype(F32) + slope * grad_act).astype(BF16)
                gg_copy(i).start()
            staged(i, stages)
            return 0

        lax.fori_loop(0, NCH, body, 0)

    def send_first(_):
        for i in range(AHEAD):
            send_genome(i)

    up_step(0, ())
    send_c(0)
    up_step(1, ((0, send_x, 0), (4, send_first, 0), (5, send_z, 0)))
    send_c(1)

    stages = (
        (0, send_x, 1),
        (2, send_y, 0),
        (4, send_z, 1),
        (5, send_az, 0),
        (7, send_y, 1),
        (8, send_ax, 0),
        (10, send_az, 1),
        (11, send_ac, 0),
        (12, finish, 0),
        (13, send_ax, 1),
        (15, send_ac, 1),
    )

    def genome_step(i, _):
        for way in range(2):
            genome_copy(i, way).wait_recv()
        pl.when(i + AHEAD < NGC)(lambda: send_genome(i + AHEAD))
        block = ds(i * gch, gch, gch)
        a_prev = gelu(g_prev[block].astype(F32) * has_prev).astype(BF16)
        a_next = gelu(g_next[block].astype(F32) * has_next).astype(BF16)
        conv = dot(a_prev, w[0]) + dot(act[block], w[1]) + dot(a_next, w[2])
        ob[block] = (g[block].astype(F32) + conv).astype(BF16)
        out_copy(i).start()
        staged(i, stages)
        return 0

    lax.fori_loop(0, NGC, genome_step, 0)
    finish(1)

    def drain_up(i, _):
        for way in range(2):
            for j in range(2):
                up_copy(j, i, way).wait_send()
        gg_copy(i).wait()
        return 0

    lax.fori_loop(0, NCH, drain_up, 0)

    def drain_genome(i, _):
        for way in range(2):
            genome_copy(i, way).wait_send()
        out_copy(i).wait()
        return 0

    lax.fori_loop(0, NGC, drain_genome, 0)
    for j in range(2):
        for k in range(nx):
            c_copy(j, k).wait_send()
        for k in range(nx - 1):
            x_copy(j, k).wait_send()
            ax_copy(j, k, x).wait_send()
        for k in range(nz - 1):
            z_copy(j, k).wait_send()
            az_copy(j, k, z).wait_send()
        for k in range(ny - 1):
            y_copy(j, k, y).wait_send()
        ac_copy(j, core).wait_send()
        gw_copy(j).wait()


def per_device(dims, genome, conv_weight, upstream):
    nz, nxl, ny, nd = dims
    nx = nxl * nd
    _, bins, chans = genome.shape
    rows, half = 3 * chans, chans // 4
    hop = DILATION_BINS // bins
    dma = pltpu.SemaphoreType.DMA
    block = pltpu.VMEM((bins, chans), BF16)
    out, grad_genome, grad_weight = pl.pallas_call(
        functools.partial(kernel, dims, hop),
        out_shape=(
            jax.ShapeDtypeStruct((bins, chans), BF16),
            jax.ShapeDtypeStruct((bins, chans), BF16),
            jax.ShapeDtypeStruct((3, chans, chans), F32),
        ),
        in_specs=[pl.BlockSpec(memory_space=pl.ANY)] * 3,
        out_specs=(pl.BlockSpec(memory_space=pl.ANY),) * 3,
        scratch_shapes=[
            block, block,
            pltpu.VMEM((3, chans, chans), BF16),
            block, block, block, block, block,
            pltpu.VMEM((chans, bins), BF16),
            block, block,
            pltpu.VMEM((2, 2, rows, half), F32),
            pltpu.VMEM((2, rows, half), F32),
            pltpu.VMEM((2, rows, half), BF16),
            pltpu.VMEM((2, nx - 1, rows // nx, half), BF16),
            pltpu.VMEM((2, rows // nx, half), F32),
            pltpu.VMEM((2, nz - 1, rows // nx // nz, half), F32),
            pltpu.VMEM((2, ny, rows // nx // nz, half), F32),
            pltpu.VMEM((2, 2, rows, half), BF16),
            pltpu.VMEM((3, chans, chans), F32),
            dma((3,)),
            dma((2, 2, NCH)), dma((2, 2, NCH)),
            dma((2, NGC)), dma((2, NGC)),
            dma((NGC,)), dma((NCH,)), dma((2,)),
            dma((2, nx)), dma((2, nx)),
            dma((2, nx - 1)), dma((2, nx - 1)),
            dma((2, nz - 1)), dma((2, nz - 1)),
            dma((2, ny - 1)), dma((2, ny - 1)),
            dma((2, nz - 1)), dma((2, nz - 1)),
            dma((2, nx - 1)), dma((2, nx - 1)),
            dma((2,)), dma((2,)),
        ],
        compiler_params=pltpu.CompilerParams(
            collective_id=0, has_side_effects=True, vmem_limit_bytes=60 * 1024 * 1024
        ),
    )(genome.reshape(bins, chans), conv_weight, upstream.reshape(bins, chans))
    return out.reshape(genome.shape), grad_genome.reshape(genome.shape), grad_weight


def solution(mesh):
    ny, nxl, nc = 4, 2, 2
    nz = mesh.shape["seq"] // (ny * nxl * nc)
    return jax.shard_map(
        functools.partial(per_device, (nz, nxl, ny, mesh.shape["dp"])),
        mesh=mesh,
        in_specs=(P("dp", "seq", None), P(), P("dp", "seq", None)),
        out_specs=(P("dp", "seq", None), P("dp", "seq", None), P()),
        check_vma=False,
    )
```

time: 358 us -> 153 us (0.43)
  the two profiles are of different devices: /device:TPU:1 before, /device:TPU:57 now
where the time goes in v1:
time: 153 us
  Pallas kernels  145 us (95%)
  local copies, waits for them, and re-layouts  7.51 us (5%)
    pallas_call x1, Pallas kernels, per_device(): pl.pallas_call(functools.partial(kernel, dims, hop), out_shape=(jax.Shape...  145 us
    unnamed x7, local copies, waits for them, and re-layouts  7.51 us

profile of v1, /device:TPU:57, one launch (start us, length us, event | category | flops | bytes accessed | tf_op | source)
XLA Modules:
  0.0 152.9 jit_solution(12093946194720117127)
XLA Ops:
  0.6 144.7 %shard_map.58 = (bf16[2048,512]{1,0:T(8,128)(2,1)}, bf16[2048,512]{1,0:T(8,128)(2,1)}, f32[3,512,512]{2,1,0:T(8,128)}) custom-call(bf16[2048,512]{1,0:T(8,128)(2,1)} %bitcast.6, bf16[3,512,512]{2,1,0:T(8,128)(2,1)} %w_hbm.1, bf16[2048,512]{1,0:T(8,128)(2,1)} %bitcast.7), custom_call_target="tpu_custom_call" | custom-call | tf_op jit(solution)/shard_map/pallas_call | solution.py:379
  145.3 0.0 copy-start.1
  145.3 3.2 %copy.9 = bf16[1,2048,512]{2,1,0:T(8,128)(2,1)} copy(bf16[1,2048,512]{2,1,0:T(8,128)(2,1)} %bitcast.5) | data formatting | bytes 4194304
  148.5 0.0 copy-done.1
  148.5 0.0 copy-start
  148.5 1.3 copy.10
  149.9 1.3 copy-done
  151.2 1.7 %copy.11 = f32[3,512,512]{2,1,0:T(8,128)} copy(f32[3,512,512]{2,1,0:T(8,128)S(1)} %copy-done) | data formatting | bytes 6291456
Async XLA Ops:
  145.3 3.2 %copy-start.1 = (bf16[2048,512]{1,0:T(8,128)(2,1)S(1)}, bf16[2048,512]{1,0:T(8,128)(2,1)}, u32[]{:S(2)}) copy-start(bf16[2048,512]{1,0:T(8,128)(2,1)} %get-tuple-element.7) | copy-start | bytes 6291460
  148.5 2.6 %copy-start = (f32[3,512,512]{2,1,0:T(8,128)S(1)}, f32[3,512,512]{2,1,0:T(8,128)}, u32[]{:S(2)}) copy-start(f32[3,512,512]{2,1,0:T(8,128)} %get-tuple-element.14) | copy-start | bytes 9437188

commit v2 on v1

v2 whole, which is shorter than its diff:
```python
import functools

import jax
import jax.numpy as jnp
from jax import lax
from jax.experimental import pallas as pl
from jax.experimental.pallas import tpu as pltpu
from jax.sharding import PartitionSpec as P

MESH = pl.DeviceIdType.MESH
F32 = jnp.float32
BF16 = jnp.bfloat16
DILATION_BINS = 4096
NCH = 4
NGC = 16
GROUPS = 4
EARLY = 4
LATE = 9
VMEM_MIB = 46
CUBIC = 0.044715
SLOPE = 0.7978845608028654


def gelu(x):
    return x * (0.5 * (1.0 + jnp.tanh(SLOPE * (x + CUBIC * (x * x * x)))))


def gelu_slope(x):
    square = x * x
    t = jnp.tanh(SLOPE * (x + CUBIC * (x * square)))
    return 0.5 * (1.0 + t) + (0.5 * SLOPE) * x * (1.0 - t * t) * (1.0 + (3.0 * CUBIC) * square)


def dot(a, b):
    return jnp.dot(a, b, preferred_element_type=F32)


def dot_nt(a, b):
    return lax.dot_general(a, b, (((1,), (1,)), ((), ())), preferred_element_type=F32)


def kernel(
    dims, hop,
    g_hbm, w_hbm, u_hbm, out_hbm, gg_hbm, gw_hbm,
    g, u, w, u_other, g_other, u_prev, u_next, g_prev, g_next, act, act_t, ob, gb,
    acc, rc, os_, orx, is_, irx, zf, zs, rz, ry, ag,
    lsem, ous, our, ogs, ogr, us, ur, gs, gr, osem, gsem, wsem,
    cs, cr, oss, osr, iss, isr, zss, zr, yss, yr, azs, azr, ais, air, aos, aor, acs, acr, ysem,
):
    nz, nxl, ny, nd = dims
    nx = nxl * nd
    ns = nz * nxl * ny * 2
    bins, chans = g.shape
    rows = 3 * chans
    rx_rows = rows // nx
    rz_rows = rx_rows // nz
    ch, gch = bins // NCH, bins // NGC
    wide = chans // GROUPS

    s = lax.axis_index("seq")
    d = lax.axis_index("dp")
    core = lax.rem(s, 2)
    y = lax.rem(lax.div(s, 2), ny)
    xl = lax.rem(lax.div(s, 2 * ny), nxl)
    z = lax.div(s, 2 * ny * nxl)
    x = d * nxl + xl
    base = s - core
    moves, sums = core == 0, core == 1

    def at(z_, x_, y_, c_):
        return {
            "dp": lax.div(x_, nxl),
            "seq": ((z_ * nxl + lax.rem(x_, nxl)) * ny + y_) * 2 + c_,
        }

    def beside(way, c_):
        return {"dp": d, "seq": lax.rem(base + (hop, ns - hop)[way], ns) + c_}

    partner = at(z, x, y, 1 - core)

    outer_x = lax.rem(x + 3 - 2 * xl, nx)
    inner_x = x + 1 - 2 * xl
    outer, inner = at(z, outer_x, y, core), at(z, inner_x, y, core)

    def z_at(k):
        return lax.rem(z + 1 + k, nz)

    def z_from(k):
        return lax.rem(z + 2 * nz - 1 - k, nz)

    def y_at(k):
        return lax.rem(y + 1 + k, ny)

    def y_from(k):
        return lax.rem(y + 2 * ny - 1 - k, ny)

    z_peers = [at(z_at(k), x, y, core) for k in range(nz - 1)]
    y_peers = [at(z, x, y_at(k), core) for k in range(ny - 1)]

    def ds(start, size, step):
        return pl.ds(pl.multiple_of(start, step), size)

    def remote(src, dst, send, recv, device):
        return pltpu.make_async_remote_copy(
            src_ref=src, dst_ref=dst, send_sem=send, recv_sem=recv, device_id=device, device_id_type=MESH
        )

    loads = [
        pltpu.make_async_copy(g_hbm, g, lsem.at[0]),
        pltpu.make_async_copy(u_hbm, u, lsem.at[1]),
        pltpu.make_async_copy(w_hbm, w, lsem.at[2]),
    ]
    for load in loads:
        load.start()

    barrier = pltpu.get_barrier_semaphore()

    def greet(devices):
        for device in devices:
            pl.semaphore_signal(barrier, inc=1, device_id=device, device_id_type=MESH)

    greet([partner, beside(0, 0), beside(1, 0)])
    sum_peers = z_peers + y_peers + [outer, inner]

    @pl.when(moves)
    def _():
        pl.semaphore_wait(barrier, 5)

    @pl.when(sums)
    def _():
        greet(sum_peers)
        pl.semaphore_wait(barrier, 1 + len(sum_peers))

    def columns(j):
        return pl.ds(j * wide, wide)

    def up_block(j, i):
        return (ds(i * ch, ch, ch), columns(j))

    def up_copy(j, i, way, c_):
        block = up_block(j, i)
        src, dst = (u_hbm, u_other)[c_], (u_prev, u_next)[way]
        return remote(
            src.at[block], dst.at[block], us.at[c_, way, j, i], ur.at[way, j, i], beside(way, c_)
        )

    def up_handed(j, i):
        block = up_block(j, i)
        return remote(u_hbm.at[block], u_other.at[block], ous.at[j, i], our.at[j, i], partner)

    def genome_copy(i, way, c_):
        block = ds(i * gch, gch, gch)
        src, dst = (g_hbm, g_other)[c_], (g_prev, g_next)[way]
        return remote(src.at[block], dst.at[block], gs.at[c_, way, i], gr.at[way, i], beside(way, c_))

    def genome_handed(i):
        block = ds(i * gch, gch, gch)
        return remote(g_hbm.at[block], g_other.at[block], ogs.at[i], ogr.at[i], partner)

    @pl.when(sums)
    def _():
        for j in range(GROUPS):

            def hand_up(i, _, j=j):
                up_handed(j, i).start()
                return 0

            lax.fori_loop(0, NCH, hand_up, 0)

        def hand_genome(i, _):
            genome_handed(i).start()
            return 0

        lax.fori_loop(0, NGC, hand_genome, 0)

    @pl.when(moves)
    def _():
        for j in range(GROUPS):

            def send_up(i, _, j=j):
                for way in range(2):
                    up_copy(j, i, way, 0).start()
                up_handed(j, i).wait_recv()
                for way in range(2):
                    up_copy(j, i, way, 1).start()
                return 0

            lax.fori_loop(0, NCH, send_up, 0)

    def x_block(x_):
        return ds(x_ * rx_rows, rx_rows, rx_rows)

    def z_block(z_):
        return ds(z_ * rz_rows, rz_rows, rz_rows)

    def c_block(k):
        return x_block((2 * (1 - d), 2 * (1 - d) + 1, inner_x, x)[k])

    def c_copy(j, k):
        block = c_block(k)
        return remote(acc.at[j, block], rc.at[j, block], cs.at[j, k], cr.at[j, k], partner)

    def o_copy(j, k):
        return remote(os_.at[j, k], orx.at[j, k], oss.at[j, k], osr.at[j, k], outer)

    def i_copy(j):
        return remote(is_.at[j], irx.at[j], iss.at[j], isr.at[j], inner)

    def z_copy(j, k):
        return remote(zs.at[j, z_block(z_at(k))], rz.at[j, k], zss.at[j, k], zr.at[j, k], z_peers[k])

    def y_copy(j, k, slot):
        return remote(ry.at[j, slot], ry.at[j, slot], yss.at[j, k], yr.at[j, k], y_peers[k])

    def az_copy(j, k, z_):
        block = ag.at[ds(x * rx_rows + z_ * rz_rows, rz_rows, rz_rows), columns(j)]
        return remote(block, block, azs.at[j, k], azr.at[j, k], z_peers[k])

    def ai_copy(j, x_):
        block = ag.at[x_block(x_), columns(j)]
        return remote(block, block, ais.at[j], air.at[j], inner)

    def ao_copy(j, k, d_):
        block = ag.at[x_block(2 * d_ + k), columns(j)]
        return remote(block, block, aos.at[j, k], aor.at[j, k], outer)

    def ac_copy(j, k, x_):
        block = ag.at[x_block(x_), columns(j)]
        return remote(block, block, acs.at[j, k], acr.at[j, k], partner)

    def send_c(j):
        @pl.when(moves)
        def _():
            for k in range(nx):
                c_copy(j, k).start()

    def send_o(j):
        for k in range(2):
            c_copy(j, k).wait_recv()
            block = c_block(k)
            os_[j, k] = acc[j, block] + rc[j, block]
            o_copy(j, k).start()

    def send_i(j):
        c_copy(j, 2).wait_recv()
        o_copy(j, 1 - xl).wait_recv()
        block = c_block(2)
        is_[j] = (acc[j, block] + rc[j, block] + orx[j, 1 - xl]).astype(BF16)
        i_copy(j).start()

    def send_z(j):
        c_copy(j, 3).wait_recv()
        o_copy(j, xl).wait_recv()
        i_copy(j).wait_recv()
        block = c_block(3)
        total = acc[j, block] + rc[j, block] + orx[j, xl] + irx[j].astype(F32)
        zf[j] = total
        zs[j] = total.astype(BF16)
        for k in range(nz - 1):
            z_copy(j, k).start()

    def send_y(j):
        for k in range(nz - 1):
            z_copy(j, k).wait_recv()
        total = zf[j, z_block(z)]
        for k in range(nz - 1):
            total += rz[j, k].astype(F32)
        ry[j, y] = total
        for k in range(ny - 1):
            y_copy(j, k, y).start()
        pl.semaphore_signal(ysem.at[j], inc=1, device_id=partner, device_id_type=MESH)

    def send_az(j):
        for k in range(ny - 1):
            y_copy(j, k, y_from(k)).wait_recv()
        total = ry[j, 0]
        for k in range(1, ny):
            total += ry[j, k]
        ag[ds(x * rx_rows + z * rz_rows, rz_rows, rz_rows), columns(j)] = total.astype(BF16)
        for k in range(nz - 1):
            az_copy(j, k, z).start()

    def send_ai(j):
        for k in range(nz - 1):
            az_copy(j, k, z_from(k)).wait_recv()
        ai_copy(j, x).start()
        ao_copy(j, xl, d).start()
        ac_copy(j, 3, x).start()

    def send_ao(j):
        ai_copy(j, inner_x).wait_recv()
        ao_copy(j, 1 - xl, d).start()
        ac_copy(j, 2, inner_x).start()

    def send_ac(j):
        for k in range(2):
            ao_copy(j, k, 1 - d).wait_recv()
            ac_copy(j, k, 2 * (1 - d) + k).start()

    def gw_copy(j):
        return pltpu.make_async_copy(ag.at[:, columns(j)], gw_hbm.at[:, columns(j)], wsem.at[j])

    def finish(j):
        @pl.when(moves)
        def _():
            for k, x_ in enumerate((2 * (1 - d), 2 * (1 - d) + 1, inner_x, x)):
                ac_copy(j, k, x_).wait_recv()

        gw_copy(j).start()

    has_prev = jnp.where(s >= hop, 1.0, 0.0).astype(F32)
    has_next = jnp.where(s < ns - hop, 1.0, 0.0).astype(F32)

    for load in loads:
        load.wait()
    acc[...] = jnp.zeros_like(acc)

    def own(i, _):
        block = ds(i * gch, gch, gch)
        a = gelu(g[block].astype(F32))
        act[block] = a.astype(BF16)
        act_t[:, block] = a.T.astype(BF16)
        return 0

    lax.fori_loop(0, NGC, own, 0)

    def send_genome(i, _):
        for way in range(2):
            genome_copy(i, way, 0).start()
        genome_handed(i).wait_recv()
        for way in range(2):
            genome_copy(i, way, 1).start()
        return 0

    @pl.when(moves)
    def _():
        lax.fori_loop(0, EARLY, send_genome, 0)

    def go_on(first, last, groups):
        for j in groups:
            pl.semaphore_wait(ysem.at[j], 1)
        lax.fori_loop(first, last, send_genome, 0)

    def masked(ref, index, there):
        value = ref[index]
        return value * jnp.full(value.shape, there, F32).astype(BF16)

    def gg_copy(i):
        block = ds(i * ch, ch, ch)
        return pltpu.make_async_copy(gb.at[block], gg_hbm.at[block], gsem.at[i])

    def out_copy(i):
        block = ds(i * gch, gch, gch)
        return pltpu.make_async_copy(ob.at[block], out_hbm.at[block], osem.at[i])

    def staged(i, stages):
        for tick, stage, groups in stages:
            when = i == tick
            if stage is not finish:
                when = jnp.logical_and(when, sums)

            @pl.when(when)
            def _(stage=stage, groups=groups):
                for j in groups if isinstance(groups, tuple) else (groups,):
                    stage(j)

    def up_step(j, stages):
        def body(i, _):
            for way in range(2):
                up_copy(j, i, way, 0).wait_recv()
            block, side = up_block(j, i)
            left = act_t[:, block]
            for tap, right in (
                (0, masked(u_next, (block, side), has_next)),
                (1, u[block, side]),
                (2, masked(u_prev, (block, side), has_prev)),
            ):
                acc[j, pl.ds(tap * chans, chans)] += dot(left, right)
            if j == GROUPS - 1:
                own_up = u[block]
                grad_act = (
                    dot_nt(masked(u_next, block, has_next), w[0])
                    + dot_nt(own_up, w[1])
                    + dot_nt(masked(u_prev, block, has_prev), w[2])
                )
                slope = gelu_slope(g[block].astype(F32))
                gb[block] = (own_up.astype(F32) + slope * grad_act).astype(BF16)
                gg_copy(i).start()
            staged(i, stages)
            return 0

        lax.fori_loop(0, NCH, body, 0)

    last = GROUPS - 1
    up_step(0, ())
    send_c(0)
    up_step(1, ((0, send_o, 0), (3, send_i, 0)))
    send_c(1)
    up_step(2, ((0, send_o, 1), (1, send_z, 0), (3, send_i, 1)))
    send_c(2)
    up_step(3, ((0, send_o, 2), (1, send_z, 1), (3, send_i, 2)))
    send_c(3)
    pl.when(sums)(functools.partial(send_o, last))

    stages = (
        (0, send_z, (2,)),
        (1, send_y, (0, 1)),
        (2, send_y, (2,)),
        (3, send_i, (3,)),
        (4, send_az, (0, 1, 2)),
        (5, send_z, (3,)),
        (7, send_y, (3,)),
        (7, send_ai, (0, 1, 2)),
        (9, send_az, (3,)),
        (9, send_ao, (0, 1, 2)),
        (11, send_ai, (3,)),
        (12, send_ac, (0, 1, 2)),
        (13, send_ao, (3,)),
        (14, finish, (0, 1, 2)),
        (15, send_ac, (3,)),
    )

    def genome_step(i, _):
        for way in range(2):
            genome_copy(i, way, 0).wait_recv()
        block = ds(i * gch, gch, gch)
        a_prev = gelu(g_prev[block].astype(F32) * has_prev).astype(BF16)
        a_next = gelu(g_next[block].astype(F32) * has_next).astype(BF16)
        conv = dot(a_prev, w[0]) + dot(act[block], w[1]) + dot(a_next, w[2])
        ob[block] = (g[block].astype(F32) + conv).astype(BF16)
        out_copy(i).start()
        staged(i, stages)
        pl.when(jnp.logical_and(moves, i == EARLY - 2))(functools.partial(go_on, EARLY, LATE, range(last)))
        pl.when(jnp.logical_and(moves, i == LATE - 2))(functools.partial(go_on, LATE, NGC, (last,)))
        return 0

    lax.fori_loop(0, NGC, genome_step, 0)
    finish(last)

    def drain_up(i, _):
        gg_copy(i).wait()

        @pl.when(moves)
        def _():
            for j in range(GROUPS):
                for way in range(2):
                    for c_ in range(2):
                        up_copy(j, i, way, c_).wait_send()

        @pl.when(sums)
        def _():
            for j in range(GROUPS):
                up_handed(j, i).wait_send()

        return 0

    lax.fori_loop(0, NCH, drain_up, 0)

    def drain_genome(i, _):
        out_copy(i).wait()

        @pl.when(moves)
        def _():
            for way in range(2):
                for c_ in range(2):
                    genome_copy(i, way, c_).wait_send()

        @pl.when(sums)
        def _():
            genome_handed(i).wait_send()

        return 0

    lax.fori_loop(0, NGC, drain_genome, 0)

    @pl.when(moves)
    def _():
        for j in range(GROUPS):
            for k in range(nx):
                c_copy(j, k).wait_send()

    @pl.when(sums)
    def _():
        for j in range(GROUPS):
            for k in range(2):
                o_copy(j, k).wait_send()
                ao_copy(j, k, d).wait_send()
            i_copy(j).wait_send()
            ai_copy(j, x).wait_send()
            for k, x_ in enumerate((2 * (1 - d), 2 * (1 - d) + 1, inner_x, x)):
                ac_copy(j, k, x_).wait_send()
            for k in range(nz - 1):
                z_copy(j, k).wait_send()
                az_copy(j, k, z).wait_send()
            for k in range(ny - 1):
                y_copy(j, k, y).wait_send()

    for j in range(GROUPS):
        gw_copy(j).wait()


def per_device(dims, genome, conv_weight, upstream):
    nz, nxl, ny, nd = dims
    nx = nxl * nd
    _, bins, chans = genome.shape
    rows, wide = 3 * chans, chans // GROUPS
    hop = DILATION_BINS // bins
    dma = pltpu.SemaphoreType.DMA
    block = pltpu.VMEM((bins, chans), BF16)
    out, grad_genome, grad_weight = pl.pallas_call(
        functools.partial(kernel, dims, hop),
        out_shape=(
            jax.ShapeDtypeStruct((bins, chans), BF16),
            jax.ShapeDtypeStruct((bins, chans), BF16),
            jax.ShapeDtypeStruct((rows, chans), BF16),
        ),
        in_specs=[pl.BlockSpec(memory_space=pltpu.HBM)] * 3,
        out_specs=(pl.BlockSpec(memory_space=pl.ANY),) * 3,
        scratch_shapes=[
            block, block,
            pltpu.VMEM((3, chans, chans), BF16),
            block, block, block, block, block, block, block,
            pltpu.VMEM((chans, bins), BF16),
            block, block,
            pltpu.VMEM((GROUPS, rows, wide), F32),
            pltpu.VMEM((GROUPS, rows, wide), F32),
            pltpu.VMEM((GROUPS, 2, rows // nx, wide), F32),
            pltpu.VMEM((GROUPS, 2, rows // nx, wide), F32),
            pltpu.VMEM((GROUPS, rows // nx, wide), BF16),
            pltpu.VMEM((GROUPS, rows // nx, wide), BF16),
            pltpu.VMEM((GROUPS, rows // nx, wide), F32),
            pltpu.VMEM((GROUPS, rows // nx, wide), BF16),
            pltpu.VMEM((GROUPS, nz - 1, rows // nx // nz, wide), BF16),
            pltpu.VMEM((GROUPS, ny, rows // nx // nz, wide), F32),
            pltpu.VMEM((rows, chans), BF16),
            dma((3,)),
            dma((GROUPS, NCH)), dma((GROUPS, NCH)),
            dma((NGC,)), dma((NGC,)),
            dma((2, 2, GROUPS, NCH)), dma((2, GROUPS, NCH)),
            dma((2, 2, NGC)), dma((2, NGC)),
            dma((NGC,)), dma((NCH,)), dma((GROUPS,)),
            dma((GROUPS, nx)), dma((GROUPS, nx)),
            dma((GROUPS, 2)), dma((GROUPS, 2)),
            dma((GROUPS,)), dma((GROUPS,)),
            dma((GROUPS, nz - 1)), dma((GROUPS, nz - 1)),
            dma((GROUPS, ny - 1)), dma((GROUPS, ny - 1)),
            dma((GROUPS, nz - 1)), dma((GROUPS, nz - 1)),
            dma((GROUPS,)), dma((GROUPS,)),
            dma((GROUPS, 2)), dma((GROUPS, 2)),
            dma((GROUPS, nx)), dma((GROUPS, nx)),
            pltpu.SemaphoreType.REGULAR((GROUPS,)),
        ],
        compiler_params=pltpu.CompilerParams(
            collective_id=0, has_side_effects=True, vmem_limit_bytes=VMEM_MIB * 1024 * 1024
        ),
    )(*(pltpu.with_memory_space_constraint(a, pltpu.HBM) for a in (genome[0], conv_weight, upstream[0])))
    return out[None], grad_genome[None], grad_weight.reshape(3, chans, chans).astype(F32)


def solution(mesh):
    ny, nxl, nc = 4, 2, 2
    nz = mesh.shape["seq"] // (ny * nxl * nc)
    return jax.shard_map(
        functools.partial(per_device, (nz, nxl, ny, mesh.shape["dp"])),
        mesh=mesh,
        in_specs=(P("dp", "seq", None), P(), P("dp", "seq", None)),
        out_specs=(P("dp", "seq", None), P("dp", "seq", None), P()),
        check_vma=False,
    )
```

time: 153 us -> 137 us (0.90)
  the two profiles are of different devices: /device:TPU:57 before, /device:TPU:1 now
where the time goes in v2:
time: 137 us
  Pallas kernels  132 us (96%)
  local copies, waits for them, and re-layouts  2.64 us (2%)
  other arithmetic  2.11 us (2%)
    pallas_call x1, Pallas kernels, per_device(): pl.pallas_call(functools.partial(kernel, dims, hop), out_shape=(jax.Shape...  132 us

profile of v2, /device:TPU:1, one launch (start us, length us, event | category | flops | bytes accessed | tf_op | source)
XLA Modules:
  0.0 137.3 jit_solution(8286540256252749230)
XLA Ops:
  0.6 131.9 %shard_map.58 = (bf16[2048,512]{1,0:T(8,128)(2,1)S(1)}, bf16[2048,512]{1,0:T(8,128)(2,1)S(1)}, bf16[1536,512]{1,0:T(8,128)(2,1)S(1)}) custom-call(bf16[2048,512]{1,0:T(8,128)(2,1)} %bitcast.9, bf16[3,512,512]{2,1,0:T(8,128)(2,1)} %w_hbm.1, bf16[2048,512]{1,0:T(8,128)(2,1)} %bitcast.10), custom_call_target="tpu_custom_call" | custom-call | tf_op jit(solution)/shard_map/pallas_call | solution.py:510
  132.5 2.1 %convert.1 = f32[3,512,512]{2,1,0:T(8,128)} convert(bf16[3,512,512]{2,1,0:T(8,128)(2,1)S(1)} %bitcast.8) | non-fusion elementwise | flops 786432 | bytes 4718592 | tf_op jit(solution)/shard_map/convert_element_type | solution.py:557
  134.7 1.3 copy.8
  136.0 1.3 copy.9

commit v3 on v2

--- a/solution.py
+++ b/solution.py
@@ -14,8 +14,7 @@
 NCH = 4
 NGC = 16
 GROUPS = 4
-EARLY = 4
-LATE = 9
+AHEAD = 4
 VMEM_MIB = 46
 CUBIC = 0.044715
 SLOPE = 0.7978845608028654
@@ -43,9 +42,9 @@
     dims, hop,
     g_hbm, w_hbm, u_hbm, out_hbm, gg_hbm, gw_hbm,
     g, u, w, u_other, g_other, u_prev, u_next, g_prev, g_next, act, act_t, ob, gb,
-    acc, rc, os_, orx, is_, irx, zf, zs, rz, ry, ag,
+    acc, rc, os_, orx, is_, irx, zf, zs, rz, ry, yh, ag,
     lsem, ous, our, ogs, ogr, us, ur, gs, gr, osem, gsem, wsem,
-    cs, cr, oss, osr, iss, isr, zss, zr, yss, yr, azs, azr, ais, air, aos, aor, acs, acr, ysem,
+    cs, cr, oss, osr, iss, isr, zss, zr, yss, yr, azs, azr, ais, air, aos, aor, acs, acr, yhs, yhr,
 ):
     nz, nxl, ny, nd = dims
     nx = nxl * nd
@@ -95,7 +94,8 @@
         return lax.rem(y + 2 * ny - 1 - k, ny)
 
     z_peers = [at(z_at(k), x, y, core) for k in range(nz - 1)]
-    y_peers = [at(z, x, y_at(k), core) for k in range(ny - 1)]
+    y_peers = [at(z, x, y_at(k), 1) for k in range(ny - 1)]
+    y_movers = [at(z, x, y_at(k), 0) for k in range(ny - 1)]
 
     def ds(start, size, step):
         return pl.ds(pl.multiple_of(start, step), size)
@@ -120,15 +120,15 @@
             pl.semaphore_signal(barrier, inc=1, device_id=device, device_id_type=MESH)
 
     greet([partner, beside(0, 0), beside(1, 0)])
-    sum_peers = z_peers + y_peers + [outer, inner]
+    sum_peers = z_peers + [outer, inner]
 
     @pl.when(moves)
     def _():
-        pl.semaphore_wait(barrier, 5)
+        pl.semaphore_wait(barrier, 5 + len(y_movers))
 
     @pl.when(sums)
     def _():
-        greet(sum_peers)
+        greet(sum_peers + y_movers)
         pl.semaphore_wait(barrier, 1 + len(sum_peers))
 
     def columns(j):
@@ -210,7 +210,10 @@
         return remote(zs.at[j, z_block(z_at(k))], rz.at[j, k], zss.at[j, k], zr.at[j, k], z_peers[k])
 
     def y_copy(j, k, slot):
-        return remote(ry.at[j, slot], ry.at[j, slot], yss.at[j, k], yr.at[j, k], y_peers[k])
+        return remote(yh.at[j], ry.at[j, slot], yss.at[j, k], yr.at[j, k], y_peers[k])
+
+    def y_handed(j):
+        return remote(ry.at[j, y], yh.at[j], yhs.at[j], yhr.at[j], partner)
 
     def az_copy(j, k, z_):
         block = ag.at[ds(x * rx_rows + z_ * rz_rows, rz_rows, rz_rows), columns(j)]
@@ -266,9 +269,12 @@
         for k in range(nz - 1):
             total += rz[j, k].astype(F32)
         ry[j, y] = total
+        y_handed(j).start()
+
+    def pass_y(j):
+        y_handed(j).wait_recv()
         for k in range(ny - 1):
             y_copy(j, k, y).start()
-        pl.semaphore_signal(ysem.at[j], inc=1, device_id=partner, device_id_type=MESH)
 
     def send_az(j):
         for k in range(ny - 1):
@@ -334,12 +340,7 @@
 
     @pl.when(moves)
     def _():
-        lax.fori_loop(0, EARLY, send_genome, 0)
-
-    def go_on(first, last, groups):
-        for j in groups:
-            pl.semaphore_wait(ysem.at[j], 1)
-        lax.fori_loop(first, last, send_genome, 0)
+        lax.fori_loop(0, AHEAD, send_genome, 0)
 
     def masked(ref, index, there):
         value = ref[index]
@@ -356,8 +357,7 @@
     def staged(i, stages):
         for tick, stage, groups in stages:
             when = i == tick
-            if stage is not finish:
-                when = jnp.logical_and(when, sums)
+            when = jnp.logical_and(when, moves if stage is pass_y else sums)
 
             @pl.when(when)
             def _(stage=stage, groups=groups):
@@ -404,25 +404,28 @@
 
     stages = (
         (0, send_z, (2,)),
-        (1, send_y, (0, 1)),
-        (2, send_y, (2,)),
+        (2, send_y, (0, 1, 2)),
+        (3, pass_y, (0, 1, 2)),
         (3, send_i, (3,)),
-        (4, send_az, (0, 1, 2)),
         (5, send_z, (3,)),
         (7, send_y, (3,)),
-        (7, send_ai, (0, 1, 2)),
-        (9, send_az, (3,)),
-        (9, send_ao, (0, 1, 2)),
-        (11, send_ai, (3,)),
-        (12, send_ac, (0, 1, 2)),
-        (13, send_ao, (3,)),
-        (14, finish, (0, 1, 2)),
-        (15, send_ac, (3,)),
+        (7, pass_y, (3,)),
+        (9, send_az, (0, 1, 2)),
+        (11, send_ai, (0, 1, 2)),
+        (13, send_ao, (0, 1, 2)),
+        (13, send_az, (3,)),
+        (15, send_ac, (0, 1, 2)),
+        (15, send_ai, (3,)),
     )
 
     def genome_step(i, _):
         for way in range(2):
             genome_copy(i, way, 0).wait_recv()
+
+        @pl.when(jnp.logical_and(moves, i + AHEAD < NGC))
+        def _():
+            send_genome(i + AHEAD, 0)
+
         block = ds(i * gch, gch, gch)
         a_prev = gelu(g_prev[block].astype(F32) * has_prev).astype(BF16)
         a_next = gelu(g_next[block].astype(F32) * has_next).astype(BF16)
@@ -430,12 +433,17 @@
         ob[block] = (g[block].astype(F32) + conv).astype(BF16)
         out_copy(i).start()
         staged(i, stages)
-        pl.when(jnp.logical_and(moves, i == EARLY - 2))(functools.partial(go_on, EARLY, LATE, range(last)))
-        pl.when(jnp.logical_and(moves, i == LATE - 2))(functools.partial(go_on, LATE, NGC, (last,)))
         return 0
 
     lax.fori_loop(0, NGC, genome_step, 0)
-    finish(last)
+
+    @pl.when(sums)
+    def _():
+        send_ao(last)
+        send_ac(last)
+
+    for j in range(GROUPS):
+        finish(j)
 
     def drain_up(i, _):
         gg_copy(i).wait()
@@ -478,6 +486,8 @@
         for j in range(GROUPS):
             for k in range(nx):
                 c_copy(j, k).wait_send()
+            for k in range(ny - 1):
+                y_copy(j, k, y).wait_send()
 
     @pl.when(sums)
     def _():
@@ -492,8 +502,7 @@
             for k in range(nz - 1):
                 z_copy(j, k).wait_send()
                 az_copy(j, k, z).wait_send()
-            for k in range(ny - 1):
-                y_copy(j, k, y).wait_send()
+            y_handed(j).wait_send()
 
     for j in range(GROUPS):
         gw_copy(j).wait()
@@ -532,6 +541,7 @@
             pltpu.VMEM((GROUPS, rows // nx, wide), BF16),
             pltpu.VMEM((GROUPS, nz - 1, rows // nx // nz, wide), BF16),
             pltpu.VMEM((GROUPS, ny, rows // nx // nz, wide), F32),
+            pltpu.VMEM((GROUPS, rows // nx // nz, wide), F32),
             pltpu.VMEM((rows, chans), BF16),
             dma((3,)),
             dma((GROUPS, NCH)), dma((GROUPS, NCH)),
@@ -548,7 +558,7 @@
             dma((GROUPS,)), dma((GROUPS,)),
             dma((GROUPS, 2)), dma((GROUPS, 2)),
             dma((GROUPS, nx)), dma((GROUPS, nx)),
-            pltpu.SemaphoreType.REGULAR((GROUPS,)),
+            dma((GROUPS,)), dma((GROUPS,)),
         ],
         compiler_params=pltpu.CompilerParams(
             collective_id=0, has_side_effects=True, vmem_limit_bytes=VMEM_MIB * 1024 * 1024

time: 137 us -> 135 us (0.985)
  Pallas kernels: 132 us -> 129 us
    pallas_call x1, Pallas kernels: 132 us -> 129 us  [per_device(): pl.pallas_call(functools.partial(kernel, dims, hop), out_shape=(jax.Shape...]
where the time goes in v3:
time: 135 us
  Pallas kernels  129 us (96%)
  local copies, waits for them, and re-layouts  2.64 us (2%)
  other arithmetic  2.11 us (2%)
    pallas_call x1, Pallas kernels, per_device(): pl.pallas_call(functools.partial(kernel, dims, hop), out_shape=(jax.Shape...  129 us

profile of v3, /device:TPU:1, one launch (start us, length us, event | category | flops | bytes accessed | tf_op | source)
XLA Modules:
  0.0 134.7 jit_solution(6866777124680553626)
XLA Ops:
  0.6 129.3 %shard_map.58 = (bf16[2048,512]{1,0:T(8,128)(2,1)S(1)}, bf16[2048,512]{1,0:T(8,128)(2,1)S(1)}, bf16[1536,512]{1,0:T(8,128)(2,1)S(1)}) custom-call(bf16[2048,512]{1,0:T(8,128)(2,1)} %bitcast.9, bf16[3,512,512]{2,1,0:T(8,128)(2,1)} %w_hbm.1, bf16[2048,512]{1,0:T(8,128)(2,1)} %bitcast.10), custom_call_target="tpu_custom_call" | custom-call | tf_op jit(solution)/shard_map/pallas_call | solution.py:519
  130.0 2.1 %convert.1 = f32[3,512,512]{2,1,0:T(8,128)} convert(bf16[3,512,512]{2,1,0:T(8,128)(2,1)S(1)} %bitcast.8) | non-fusion elementwise | flops 786432 | bytes 4718592 | tf_op jit(solution)/shard_map/convert_element_type | solution.py:567
  132.1 1.3 copy.8
  133.4 1.3 copy.9
